TPU v7x, 32 devices: a whole 2x2x4 slice. The times are simulated.
32 devices in a mesh: groups: 2 (over x), seq: 8 (over z, y), sub: 2 (over core).
Axes of the slice: x: 2, y: 2, z: 4, core: 2. Of those that a mesh axis runs over, the one named last changes fastest.
Arguments:
- frames: bfloat16 [2048, 1024], P(('groups', 'seq', 'sub')), parts along dimension 0, may hold values from -6 to 6
- fine_gain: float32 [1024], replicated, may hold values from 0.1 to 1.9
- dw_kernel: bfloat16 [5, 1024], replicated, may hold values from -3 to 3
- w_down: bfloat16 [4096, 4096], P(None, 'seq'), may hold values from -0.21875 to 0.21875
- coarse_gain: float32 [4096], replicated, may hold values from 0.1 to 1.9
- w_qkv: bfloat16 [3, 4096, 4096], P(None, None, 'seq'), may hold values from -1.609375 to 1.609375
- w_out: bfloat16 [4096, 4096], P('seq'), may hold values from -0.09375 to 0.09375
- w_up: bfloat16 [4096, 4096], P('seq'), may hold values from -0.09375 to 0.09375
Outputs:
- denoised: bfloat16 [2048, 1024], P(('groups', 'seq', 'sub')), parts along dimension 0
There are 2 independent parts, one for each index of `groups`. A program takes and returns all parts, laid end to end along the dimension named above; an argument that names none is the same for every part. Nothing has to cross between parts.
All inputs are finite; a program needn't handle non-finite values.
Results may differ from a plain program's by a relative error of at most 0.012.
Values may be sent and summed in bfloat16 or wider, within the bound.
No kernel may reach another device: no remote copies, remote signals or barrier semaphores. Data moves between devices by JAX's collectives and lax.ppermute only.
A program may use at most 128 MiB of HBM per device.

v0:
```python
import math
import jax
import jax.numpy as jnp
from jax import lax
from jax.sharding import PartitionSpec as P

DF = 1024
HD = 128
KW = 5
epsilon = 1e-06


def padded_2(array, sides, width):
    for axis, dim in sides:
        size, length = (lax.axis_size(axis), array.shape[dim])
        up = [(i, (i + 1) % size) for i in range(size - 1)]
        down = [(j, i) for i, j in up]
        last = lax.slice_in_dim(array, length - width, length, axis=dim)
        leading = lax.slice_in_dim(array, 0, width, axis=dim)
        before = lax.ppermute(last, axis, up)
        after = lax.ppermute(leading, axis, down)
        array = jnp.concatenate([before, array, after], axis=dim)
    return array


def partner(value, axis, bit):
    mask = 2**bit
    pairs = [(source, source ^ mask) for source in range(lax.axis_size(axis))]
    return lax.ppermute(value, axis, pairs)


def attend(queries, keys_all, values_all, heads_here):
    row_total = queries.shape[0]
    block_rows = min(row_total, 512)
    key_heads = keys_all.reshape(keys_all.shape[0], heads_here, HD)
    value_heads = values_all.reshape(values_all.shape[0], heads_here, HD)
    query_blocks = queries.reshape(row_total // block_rows, block_rows, heads_here, HD)
    score_scale = 1.0 / math.sqrt(HD)

    def one_block(query_block):
        scores = (
            jnp.einsum("qhd,khd->hqk", query_block, key_heads, preferred_element_type=jnp.float32)
            * score_scale
        )
        peak = jnp.max(scores, axis=2, keepdims=True)
        weights = jnp.exp(scores - peak)
        weights = (weights / jnp.sum(weights, axis=2, keepdims=True)).astype(jnp.bfloat16)
        return jnp.einsum(
            "hqk,khd->qhd", weights, value_heads, preferred_element_type=jnp.float32
        ).astype(jnp.bfloat16)

    outputs = lax.map(one_block, query_blocks)
    return outputs.reshape(row_total, heads_here * HD)


def per_device(frames, fine_gain, dw_kernel, w_down, coarse_gain, w_qkv, w_out, w_up):
    frame_rows = frames.shape[0]
    heads_here = w_qkv.shape[2] // HD
    frames_f32 = frames.astype(jnp.float32)
    normed_fine = (
        frames_f32
        * lax.rsqrt(jnp.mean(frames_f32 * frames_f32, axis=1, keepdims=True) + epsilon)
        * fine_gain
    ).astype(jnp.bfloat16)
    padded = padded_2(normed_fine, ((("seq", "sub"), 0),), KW // 2)
    convolved = jnp.zeros((frame_rows, DF), jnp.float32)
    for offset in range(KW):
        convolved = convolved + padded[offset : offset + frame_rows].astype(
            jnp.float32
        ) * dw_kernel[offset].astype(jnp.float32)
    patches = convolved.astype(jnp.bfloat16).reshape(frame_rows // 4, 4 * DF)
    coarse = jnp.dot(
        lax.all_gather(patches, "seq", axis=0, tiled=True),
        w_down,
        preferred_element_type=jnp.float32,
    ).astype(jnp.bfloat16)
    coarse_f32 = coarse.astype(jnp.float32)
    whole = lax.all_gather(coarse, "seq", axis=1, tiled=True).astype(jnp.float32)
    normed_coarse = (
        whole * lax.rsqrt(jnp.mean(whole * whole, axis=1, keepdims=True) + epsilon) * coarse_gain
    ).astype(jnp.bfloat16)
    queries = jnp.dot(normed_coarse, w_qkv[0], preferred_element_type=jnp.float32).astype(
        jnp.bfloat16
    )
    own_keys = jnp.dot(normed_coarse, w_qkv[1], preferred_element_type=jnp.float32).astype(
        jnp.bfloat16
    )
    own_values = jnp.dot(normed_coarse, w_qkv[2], preferred_element_type=jnp.float32).astype(
        jnp.bfloat16
    )
    other_keys, other_values = partner((own_keys, own_values), "sub", 0)
    keys_all = jnp.concatenate([own_keys, other_keys], axis=0)
    values_all = jnp.concatenate([own_values, other_values], axis=0)
    attended = attend(queries, keys_all, values_all, heads_here)
    partial_out = jnp.dot(attended, w_out, preferred_element_type=jnp.float32)
    projected = lax.psum_scatter(
        partial_out.astype(jnp.bfloat16), "seq", scatter_dimension=1, tiled=True
    ).astype(jnp.float32)
    mixed = (coarse_f32 + projected).astype(jnp.bfloat16)
    lifted = lax.psum_scatter(
        jnp.dot(mixed, w_up, preferred_element_type=jnp.float32),
        "seq",
        scatter_dimension=0,
        tiled=True,
    )
    return (frames_f32 + lifted.reshape(frame_rows, DF)).astype(jnp.bfloat16)


def solution(mesh):
    placed = (
        P(("groups", "seq", "sub"), None),
        P(),
        P(),
        P(None, "seq"),
        P(),
        P(None, None, "seq"),
        P("seq", None),
        P("seq", None),
    )
    return jax.shard_map(
        per_device,
        mesh=mesh,
        in_specs=placed,
        out_specs=P(("groups", "seq", "sub"), None),
        check_vma=False,
    )
```

profile of v0, /device:TPU:0, one launch (start us, length us, event | category | flops | bytes accessed | tf_op | source)
XLA Modules:
  0.0 262.8 jit_solution(18423422648642373346)
XLA Ops:
  6.5 1.0 fusion.27
  7.6 1.0 fusion.29
  8.6 2.4 collective-permute-start
  11.0 1.3 collective-permute-start.1
  12.3 0.9 slice_convert_fusion.4
  13.2 3.0 %collective-permute-done.1 = bf16[2,1024]{1,0:T(2,128)(2,1)S(1)} collective-permute-done((bf16[2,1024]{1,0:T(2,128)(2,1)S(1)}, bf16[2,1024]{1,0:T(2,128)(2,1)S(1)}, u32[]{:S(2)}, u32[]{:S(2)}) %collective-permute-start.1) | collective-permute-done | bytes 4128 | tf_op jit(solution)/shard_map/ppermute | solution.py:21
  16.2 0.2 add_convert_fusion.1
  16.4 0.7 reshape.38
  17.1 0.0 all-gather.3.cloned.1.call-update
  17.1 0.0 all-gather.5.cloned.1.call-start
  17.2 43.4 %all-gather.3.cloned.1.call-done = bf16[128,4096]{1,0:T(8,128)(2,1)} async-done(((bf16[16,4096]{1,0:T(8,128)(2,1)}), bf16[128,4096]{1,0:T(8,128)(2,1)}) %all-gather.3.cloned.1.call-update) | async-done | bytes 1048592 | tf_op jit(solution)/shard_map/all_gather | solution.py:73
  60.6 3.9 %convolution_convert_fusion.2 = bf16[128,512]{1,0:T(8,128)(2,1)} fusion(bf16[128,4096]{1,0:T(8,128)(2,1)} %all-gather.3.cloned.1.call-done, bf16[4096,512]{1,0:T(8,128)(2,1)} %param.11), kind=kOutput, calls=%fused_computation.23 | convolution fusion | flops 536936448 | bytes 5373952 | tf_op jit(solution)/shard_map/dot_general | solution.py:72
  64.5 0.0 all-gather.5.cloned.1.call-update
  64.5 0.0 reduce-scatter.3.cloned.1.call-start
  64.6 38.4 %all-gather.5.cloned.1.call-done = bf16[128,4096]{1,0:T(8,128)(2,1)} async-done(((bf16[128,512]{1,0:T(8,128)(2,1)}), bf16[128,4096]{1,0:T(8,128)(2,1)}) %all-gather.5.cloned.1.call-update) | async-done | bytes 1048592 | tf_op jit(solution)/shard_map/all_gather | solution.py:78
  103.0 1.6 fusion.10
  104.6 3.3 %fusion.15 = bf16[128,512]{1,0:T(8,128)(2,1)S(1)} fusion(bf16[3,4096,512]{2,1,0:T(8,128)(2,1)} %param.13, bf16[128,4096]{1,0:T(8,128)(2,1)} %all-gather.5.cloned.1.call-done, f32[4096]{0:T(1024)S(1)} %copy-done.3, f32[128]{0:T(128)S(1)} %add_rsqrt_fusion), kind=kOutput, calls=%fused_computation.19 | convolution fusion | flops 539033600 | bytes 5390848 | tf_op jit(solution)/shard_map/dot_general | solution.py:88
  107.9 0.1 collective-permute-start.2
  107.9 3.0 %fusion.21 = bf16[128,512]{1,0:T(8,128)(2,1)S(1)} fusion(bf16[3,4096,512]{2,1,0:T(8,128)(2,1)} %param.13, bf16[128,4096]{1,0:T(8,128)(2,1)S(1)} %copy-done.2, f32[4096]{0:T(1024)S(1)} %copy-done.3, f32[128]{0:T(128)S(1)} %add_rsqrt_fusion), kind=kOutput, calls=%fused_computation.21 | convolution fusion | flops 539033600 | bytes 5390848 | tf_op jit(solution)/shard_map/dot_general | solution.py:85
  110.9 0.6 collective-permute-start.3
  111.5 2.9 %fusion.24 = bf16[16,4,8,128]{3,2,1,0:T(8,128)(2,1)S(1)} fusion(bf16[3,4096,512]{2,1,0:T(8,128)(2,1)} %param.13, bf16[128,4096]{1,0:T(8,128)(2,1)S(1)} %copy-done.2, f32[4096]{0:T(1024)S(1)} %copy-done.3, f32[128]{0:T(128)S(1)} %add_rsqrt_fusion), kind=kOutput, calls=%fused_computation.24 | convolution fusion | flops 539033600 | bytes 5390848 | tf_op jit(solution)/shard_map/dot_general | solution.py:82
  114.5 0.1 copy.12
  114.6 0.4 fusion.49
  115.0 0.2 convolution_multiply_fusion
  115.3 1.0 convolution_convert_fusion.1
  116.3 3.9 %convolution_convert_fusion = bf16[128,4096]{1,0:T(8,128)(2,1)} fusion(bf16[128,512]{0,1:T(8,128)(2,1)S(1)} %bitcast.57, bf16[512,4096]{1,0:T(8,128)(2,1)} %param.14), kind=kOutput, calls=%fused_computation.1 | convolution fusion | flops 537395200 | bytes 5373952 | tf_op jit(solution)/shard_map/dot_general | solution.py:95
  120.3 0.0 reduce-scatter.5.cloned.1.call-start
  120.3 62.8 %reduce-scatter.3.cloned.1.call-done = bf16[128,512]{1,0:T(8,128)(2,1)} async-done(((bf16[128,4096]{1,0:T(8,128)(2,1)}), bf16[128,512]{1,0:T(8,128)(2,1)}) %reduce-scatter.3.cloned.1.call-update) | async-done | bytes 131088 | tf_op jit(solution)/shard_map/reduce_scatter | solution.py:96
  183.2 4.3 %fusion.36 = f32[128,4096]{1,0:T(8,128)} fusion(bf16[512,4096]{1,0:T(8,128)(2,1)} %param.15, bf16[128,512]{1,0:T(8,128)(2,1)} %reduce-scatter.3.cloned.1.call-done, bf16[128,512]{1,0:T(8,128)(2,1)S(1)} %copy-done.1), kind=kOutput, calls=%fused_computation.46 | convolution fusion | flops 537133056 | bytes 6553600 | tf_op jit(solution)/shard_map/dot_general | solution.py:101
  187.5 67.0 %reduce-scatter.5.cloned.1.call-done = f32[16,4096]{1,0:T(8,128)} async-done(((f32[128,4096]{1,0:T(8,128)}), f32[16,4096]{1,0:T(8,128)}) %reduce-scatter.5.cloned.1.call-update) | async-done | bytes 262160 | tf_op jit(solution)/shard_map/reduce_scatter | solution.py:100
  254.5 1.0 reshape.42
  255.5 0.7 fusion.30
  (18 shorter events, 0.1 us)
Async XLA Ops:
  6.5 98.0 %copy-start.3 = (f32[4096]{0:T(1024)S(1)}, f32[4096]{0:T(1024)}, u32[]{:S(2)}) copy-start(f32[4096]{0:T(1024)} %param.12) | copy-start | bytes 49156
  6.5 54.1 %all-gather.3.cloned.1.call-start = ((), (), s32[]{:S(2)}) async-start(), calls=%async_computation.2 | async-start | bytes 1179648 | tf_op jit(solution)/shard_map/all_gather | solution.py:73
  8.6 4.6 %collective-permute-start = (bf16[2,1024]{1,0:T(2,128)(2,1)S(1)}, bf16[2,1024]{1,0:T(2,128)(2,1)S(1)}, u32[]{:S(2)}, u32[]{:S(2)}) collective-permute-start(bf16[2,1024]{1,0:T(2,128)(2,1)S(1)} %get-tuple-element.13), channel_id=1, source_target_pairs={{0,1},{1,2},{2,3},{3,4},{4,5},{5,6},{6,7},{7,8},{8,9},{9,10},{10,1... | collective-permute-start | bytes 12296 | tf_op jit(solution)/shard_map/ppermute | solution.py:20
  11.0 5.2 %collective-permute-start.1 = (bf16[2,1024]{1,0:T(2,128)(2,1)S(1)}, bf16[2,1024]{1,0:T(2,128)(2,1)S(1)}, u32[]{:S(2)}, u32[]{:S(2)}) collective-permute-start(bf16[2,1024]{1,0:T(2,128)(2,1)S(1)} %get-tuple-element.14), channel_id=1, source_target_pairs={{1,0},{2,1},{3,2},{4,3},{5,4},{6,5},{7,6},{8,7},{9,8},{10,9},{11,1... | collective-permute-start | bytes 12296 | tf_op jit(solution)/shard_map/ppermute | solution.py:21
  17.1 85.8 %all-gather.5.cloned.1.call-start = ((), (), s32[]{:S(2)}) async-start(), calls=%async_computation.3 | async-start | bytes 1179648 | tf_op jit(solution)/shard_map/all_gather | solution.py:78
  64.5 118.6 %reduce-scatter.3.cloned.1.call-start = ((), (), s32[]{:S(2)}) async-start(), calls=%async_computation.4 | async-start | bytes 1179648 | tf_op jit(solution)/shard_map/reduce_scatter | solution.py:96
  103.0 5.0 %copy-start.2 = (bf16[128,4096]{1,0:T(8,128)(2,1)S(1)}, bf16[128,4096]{1,0:T(8,128)(2,1)}, u32[]{:S(2)}) copy-start(bf16[128,4096]{1,0:T(8,128)(2,1)} %all-gather.5.cloned.1.call-done) | copy-start | bytes 3145732
  107.9 6.6 %collective-permute-start.2 = (bf16[128,512]{1,0:T(8,128)(2,1)S(1)}, bf16[128,512]{1,0:T(8,128)(2,1)S(1)}, u32[]{:S(2)}, u32[]{:S(2)}) collective-permute-start(bf16[128,512]{1,0:T(8,128)(2,1)S(1)} %fusion.15), channel_id=1, source_target_pairs={{0,1},{1,0},{2,3},{3,2},{4,5},{5,4},{6,7},{7,6},{8,9},{9,8},{10,11... | collective-permute-start | bytes 393224 | tf_op jit(solution)/shard_map/ppermute | solution.py:29
  110.9 3.7 %collective-permute-start.3 = (bf16[128,512]{1,0:T(8,128)(2,1)S(1)}, bf16[128,512]{1,0:T(8,128)(2,1)S(1)}, u32[]{:S(2)}, u32[]{:S(2)}) collective-permute-start(bf16[128,512]{1,0:T(8,128)(2,1)S(1)} %fusion.21), channel_id=1, source_target_pairs={{0,1},{1,0},{2,3},{3,2},{4,5},{5,4},{6,7},{7,6},{8,9},{9,8},{10,11... | collective-permute-start | bytes 393224 | tf_op jit(solution)/shard_map/ppermute | solution.py:29
  115.3 67.9 %copy-start.1 = (bf16[128,512]{1,0:T(8,128)(2,1)S(1)}, bf16[128,512]{1,0:T(8,128)(2,1)}, u32[]{:S(2)}) copy-start(bf16[128,512]{1,0:T(8,128)(2,1)} %convolution_convert_fusion.2) | copy-start | bytes 393220
  120.3 135.3 %copy-start = (bf16[64,1024]{1,0:T(8,128)(2,1)S(1)}, bf16[64,1024]{1,0:T(8,128)(2,1)}, u32[]{:S(2)}) copy-start(bf16[64,1024]{1,0:T(8,128)(2,1)} %param.8) | copy-start | bytes 393220
  120.3 134.2 %reduce-scatter.5.cloned.1.call-start = ((), (), s32[]{:S(2)}) async-start(), calls=%async_computation.5 | async-start | bytes 2359296 | tf_op jit(solution)/shard_map/reduce_scatter | solution.py:100
Sparse Core Ops, SparseCore 0:
  17.3 43.2 all-gather.2
  64.6 38.2 all-gather.4
  120.4 62.7 reduce-scatter.2
  187.6 66.8 reduce-scatter.4
where the time goes:
time: 263 us
  waiting for transfers between devices  215 us (82%)
  matrix products  23 us (9%)
  between operations  13.3 us (5%)
  other arithmetic  5.48 us (2%)
  starting transfers between devices  4.4 us (2%)
    reduce_scatter x1, waiting for transfers between devices, per_device(): lax.psum_scatter(jnp.dot(mixed, w_up, preferred_element_type=jnp.float32)...  67 us
    reduce_scatter x1, waiting for transfers between devices, per_device(): lax.psum_scatter(partial_out.astype(jnp.bfloat16), 'seq', scatter_dimensi...  62.8 us
    all_gather x1, waiting for transfers between devices, per_device(): lax.all_gather(patches, 'seq', axis=0, tiled=True)  43.4 us
    all_gather x1, waiting for transfers between devices, per_device(): lax.all_gather(coarse, 'seq', axis=1, tiled=True).astype(jnp.float32)  38.4 us
  transfers between devices with their start and end apart: 8, of which 5 were waited for; matrix products, arithmetic and copies ran while one was open for 3% of the time, Pallas kernels for 0%

commit v1 on v0

--- a/solution.py
+++ b/solution.py
@@ -8,6 +8,19 @@
 HD = 128
 KW = 5
 epsilon = 1e-06
+
+
+def collect(shard, axis, dim):
+    ways = lax.axis_size(axis)
+    up = [(d, (d + 1) % ways) for d in range(ways)]
+    down = [(d, (d - 1) % ways) for d in range(ways)]
+    earlier, later = ([shard], [shard])
+    for _ in range(ways // 2):
+        earlier.append(lax.ppermute(earlier[-1], axis, up))
+    for _ in range((ways - 1) // 2):
+        later.append(lax.ppermute(later[-1], axis, down))
+    line = jnp.concatenate([*earlier[::-1], *later[1:]], axis=dim)
+    return jnp.roll(line, (lax.axis_index(axis) - ways // 2) * shard.shape[dim], axis=dim)
 
 
 def padded_2(array, sides, width):
@@ -69,11 +82,9 @@
             jnp.float32
         ) * dw_kernel[offset].astype(jnp.float32)
     patches = convolved.astype(jnp.bfloat16).reshape(frame_rows // 4, 4 * DF)
-    coarse = jnp.dot(
-        lax.all_gather(patches, "seq", axis=0, tiled=True),
-        w_down,
-        preferred_element_type=jnp.float32,
-    ).astype(jnp.bfloat16)
+    coarse = jnp.dot(collect(patches, "seq", 0), w_down, preferred_element_type=jnp.float32).astype(
+        jnp.bfloat16
+    )
     coarse_f32 = coarse.astype(jnp.float32)
     whole = lax.all_gather(coarse, "seq", axis=1, tiled=True).astype(jnp.float32)
     normed_coarse = (

time: 263 us -> 255 us (0.970)
  waiting for transfers between devices: 215 us -> 191 us
  starting transfers between devices: 4.4 us -> 20.9 us
    all_gather x1 -> x0, waiting for transfers between devices: 43.4 us -> none  [per_device(): lax.all_gather(patches, 'seq', axis=0, tiled=True)]
    ppermute x0 -> x7, waiting for transfers between devices: none -> 17.2 us  [the longest x4 16.9 us: collect(): earlier.append(lax.ppermute(earlier[-1], axis, up))]
    ppermute x0 -> x7, starting transfers between devices: none -> 16.5 us  [the longest x3 13.3 us: collect(): later.append(lax.ppermute(later[-1], axis, down))]
  transfers between devices with their start and end apart: 8 -> 14, of which waited for: 5 -> 9; matrix products, arithmetic and copies ran while one was open for 3% -> 3% of each run, Pallas kernels for 0% -> 0%
where the time goes in v1:
time: 255 us
  waiting for transfers between devices  191 us (75%)
  matrix products  22.9 us (9%)
  starting transfers between devices  20.9 us (8%)
  between operations  13.4 us (5%)
  other arithmetic  5.38 us (2%)
    reduce_scatter x1, waiting for transfers between devices, per_device(): lax.psum_scatter(jnp.dot(mixed, w_up, preferred_element_type=jnp.float32)...  66.9 us
    reduce_scatter x1, waiting for transfers between devices, per_device(): lax.psum_scatter(partial_out.astype(jnp.bfloat16), 'seq', scatter_dimensi...  63 us
    all_gather x1, waiting for transfers between devices, per_device(): lax.all_gather(coarse, 'seq', axis=1, tiled=True).astype(jnp.float32)  40.5 us
    ppermute x4, waiting for transfers between devices, collect(): earlier.append(lax.ppermute(earlier[-1], axis, up))  16.9 us
    ppermute x3, starting transfers between devices, collect(): later.append(lax.ppermute(later[-1], axis, down))  13.3 us
  transfers between devices with their start and end apart: 14, of which 9 were waited for; matrix products, arithmetic and copies ran while one was open for 3% of the time, Pallas kernels for 0%

profile of v1, /device:TPU:0, one launch (start us, length us, event | category | flops | bytes accessed | tf_op | source)
XLA Modules:
  0.0 254.6 jit_solution(14526256825828652674)
XLA Ops:
  6.5 1.0 fusion.28
  7.6 1.0 fusion.30
  8.6 2.4 collective-permute-start
  11.0 1.3 collective-permute-start.1
  12.3 0.9 slice_convert_fusion.4
  13.2 3.0 %collective-permute-done.1 = bf16[2,1024]{1,0:T(2,128)(2,1)S(1)} collective-permute-done((bf16[2,1024]{1,0:T(2,128)(2,1)S(1)}, bf16[2,1024]{1,0:T(2,128)(2,1)S(1)}, u32[]{:S(2)}, u32[]{:S(2)}) %collective-permute-start.1) | collective-permute-done | bytes 4128 | tf_op jit(solution)/shard_map/ppermute | solution.py:34
  16.5 2.3 collective-permute-start.2
  18.8 6.6 %collective-permute-done.2 = bf16[16,4096]{1,0:T(8,128)(2,1)S(1)} collective-permute-done((bf16[16,4096]{1,0:T(8,128)(2,1)S(1)}, bf16[16,4096]{1,0:T(8,128)(2,1)S(1)}, u32[]{:S(2)}, u32[]{:S(2)}) %collective-permute-start.2) | collective-permute-done | bytes 131104 | tf_op jit(solution)/shard_map/ppermute | solution.py:19
  25.4 4.7 %collective-permute-start.6 = (bf16[16,4096]{1,0:T(8,128)(2,1)S(1)}, bf16[16,4096]{1,0:T(8,128)(2,1)S(1)}, u32[]{:S(2)}, u32[]{:S(2)}) collective-permute-start(bf16[16,4096]{1,0:T(8,128)(2,1)S(1)} %reshape.38), channel_id=1, source_target_pairs={{0,14},{2,0},{4,2},{6,4},{8,6},{10,8},{12,10},{14,12},{1,15},{3,1}... | collective-permute-start | bytes 393224 | tf_op jit(solution)/shard_map/ppermute | solution.py:21
  30.2 4.1 %collective-permute-done.3 = bf16[16,4096]{1,0:T(8,128)(2,1)S(1)} collective-permute-done((bf16[16,4096]{1,0:T(8,128)(2,1)S(1)}, bf16[16,4096]{1,0:T(8,128)(2,1)S(1)}, u32[]{:S(2)}, u32[]{:S(2)}) %collective-permute-start.3) | collective-permute-done | bytes 131104 | tf_op jit(solution)/shard_map/ppermute | solution.py:19
  34.2 0.3 collective-permute-start.4
  34.5 4.4 %collective-permute-start.7 = (bf16[16,4096]{1,0:T(8,128)(2,1)S(1)}, bf16[16,4096]{1,0:T(8,128)(2,1)S(1)}, u32[]{:S(2)}, u32[]{:S(2)}) collective-permute-start(bf16[16,4096]{1,0:T(8,128)(2,1)S(1)} %collective-permute-done.6), channel_id=1, source_target_pairs={{0,14},{2,0},{4,2},{6,4},{8,6},{10,8},{12,10},{14,12},{1,15},{3,1}... | collective-permute-start | bytes 393224 | tf_op jit(solution)/shard_map/ppermute | solution.py:21
  38.9 3.2 %collective-permute-done.4 = bf16[16,4096]{1,0:T(8,128)(2,1)S(1)} collective-permute-done((bf16[16,4096]{1,0:T(8,128)(2,1)S(1)}, bf16[16,4096]{1,0:T(8,128)(2,1)S(1)}, u32[]{:S(2)}, u32[]{:S(2)}) %collective-permute-start.4) | collective-permute-done | bytes 131104 | tf_op jit(solution)/shard_map/ppermute | solution.py:19
  42.1 0.6 collective-permute-start.5
  42.7 4.1 %collective-permute-start.8 = (bf16[16,4096]{1,0:T(8,128)(2,1)S(1)}, bf16[16,4096]{1,0:T(8,128)(2,1)S(1)}, u32[]{:S(2)}, u32[]{:S(2)}) collective-permute-start(bf16[16,4096]{1,0:T(8,128)(2,1)S(1)} %collective-permute-done.7), channel_id=1, source_target_pairs={{0,14},{2,0},{4,2},{6,4},{8,6},{10,8},{12,10},{14,12},{1,15},{3,1}... | collective-permute-start | bytes 393224 | tf_op jit(solution)/shard_map/ppermute | solution.py:21
  46.8 3.0 %collective-permute-done.5 = bf16[16,4096]{1,0:T(8,128)(2,1)S(1)} collective-permute-done((bf16[16,4096]{1,0:T(8,128)(2,1)S(1)}, bf16[16,4096]{1,0:T(8,128)(2,1)S(1)}, u32[]{:S(2)}, u32[]{:S(2)}) %collective-permute-start.5) | collective-permute-done | bytes 131104 | tf_op jit(solution)/shard_map/ppermute | solution.py:19
  50.0 0.3 collective-permute-done.8
  50.5 3.7 %convolution_convert_fusion.2 = bf16[128,512]{1,0:T(8,128)(2,1)} fusion(bf16[4096,512]{1,0:T(8,128)(2,1)} %param.11, bf16[256,4096]{1,0:T(8,128)(2,1)S(1)} %constant_dynamic-update-slice_fusion, s32[]{:T(128)S(6)} %select_n.14), kind=kOutput, calls=%fused_computation.23 | convolution fusion | flops 536936448 | bytes 5373956 | tf_op jit(solution)/shard_map/dot_general | solution.py:85
  54.2 40.5 %all-gather.2.cloned.1.call-done = bf16[128,4096]{1,0:T(8,128)(2,1)} async-done(((bf16[128,512]{1,0:T(8,128)(2,1)}), bf16[128,4096]{1,0:T(8,128)(2,1)}) %all-gather.2.cloned.1.call-update) | async-done | bytes 1048592 | tf_op jit(solution)/shard_map/all_gather | solution.py:89
  94.8 1.5 fusion.10
  96.3 3.3 %fusion.21 = bf16[128,512]{1,0:T(8,128)(2,1)S(1)} fusion(bf16[3,4096,512]{2,1,0:T(8,128)(2,1)} %param.13, bf16[128,4096]{1,0:T(8,128)(2,1)} %all-gather.2.cloned.1.call-done, f32[4096]{0:T(1024)S(1)} %copy-done.3, f32[128]{0:T(128)S(1)} %add_rsqrt_fusion), kind=kOutput, calls=%fused_computation.21 | convolution fusion | flops 539033600 | bytes 5390848 | tf_op jit(solution)/shard_map/dot_general | solution.py:96
  99.7 3.0 %fusion.15 = bf16[128,512]{1,0:T(8,128)(2,1)S(1)} fusion(bf16[3,4096,512]{2,1,0:T(8,128)(2,1)} %param.13, bf16[128,4096]{1,0:T(8,128)(2,1)S(1)} %copy-done.2, f32[4096]{0:T(1024)S(1)} %copy-done.3, f32[128]{0:T(128)S(1)} %add_rsqrt_fusion), kind=kOutput, calls=%fused_computation.19 | convolution fusion | flops 539033600 | bytes 5390848 | tf_op jit(solution)/shard_map/dot_general | solution.py:99
  102.7 0.6 collective-permute-start.9
  103.3 2.9 %fusion.24 = bf16[16,4,8,128]{3,2,1,0:T(8,128)(2,1)S(1)} fusion(bf16[3,4096,512]{2,1,0:T(8,128)(2,1)} %param.13, bf16[128,4096]{1,0:T(8,128)(2,1)S(1)} %copy-done.2, f32[4096]{0:T(1024)S(1)} %copy-done.3, f32[128]{0:T(128)S(1)} %add_rsqrt_fusion), kind=kOutput, calls=%fused_computation.24 | convolution fusion | flops 539033600 | bytes 5390848 | tf_op jit(solution)/shard_map/dot_general | solution.py:93
  106.6 0.4 fusion.51
  107.1 1.1 convolution_convert_fusion.1
  108.1 3.9 %convolution_convert_fusion = bf16[128,4096]{1,0:T(8,128)(2,1)} fusion(bf16[128,512]{0,1:T(8,128)(2,1)S(1)} %bitcast.56, bf16[512,4096]{1,0:T(8,128)(2,1)} %param.14), kind=kOutput, calls=%fused_computation.1 | convolution fusion | flops 537395200 | bytes 5373952 | tf_op jit(solution)/shard_map/dot_general | solution.py:106
  112.1 63.0 %reduce-scatter.3.cloned.1.call-done = bf16[128,512]{1,0:T(8,128)(2,1)} async-done(((bf16[128,4096]{1,0:T(8,128)(2,1)}), bf16[128,512]{1,0:T(8,128)(2,1)}) %reduce-scatter.3.cloned.1.call-update) | async-done | bytes 131088 | tf_op jit(solution)/shard_map/reduce_scatter | solution.py:107
  175.1 4.3 %fusion.37 = f32[128,4096]{1,0:T(8,128)} fusion(bf16[512,4096]{1,0:T(8,128)(2,1)} %param.15, bf16[128,512]{1,0:T(8,128)(2,1)} %reduce-scatter.3.cloned.1.call-done, bf16[128,512]{1,0:T(8,128)(2,1)S(1)} %copy-done), kind=kOutput, calls=%fused_computation.47 | convolution fusion | flops 537133056 | bytes 6553600 | tf_op jit(solution)/shard_map/dot_general | solution.py:112
  179.5 66.9 %reduce-scatter.5.cloned.1.call-done = f32[16,4096]{1,0:T(8,128)} async-done(((f32[128,4096]{1,0:T(8,128)}), f32[16,4096]{1,0:T(8,128)}) %reduce-scatter.5.cloned.1.call-update) | async-done | bytes 262160 | tf_op jit(solution)/shard_map/reduce_scatter | solution.py:111
  246.4 1.0 reshape.42
  247.4 0.7 fusion.31
  (45 shorter events, 1.1 us)
Async XLA Ops:
  6.5 88.2 %all-gather.2.cloned.1.call-start = ((), (), s32[]{:S(2)}) async-start(), calls=%async_computation.2 | async-start | bytes 1179648 | tf_op jit(solution)/shard_map/all_gather | solution.py:89
  8.6 4.6 %collective-permute-start = (bf16[2,1024]{1,0:T(2,128)(2,1)S(1)}, bf16[2,1024]{1,0:T(2,128)(2,1)S(1)}, u32[]{:S(2)}, u32[]{:S(2)}) collective-permute-start(bf16[2,1024]{1,0:T(2,128)(2,1)S(1)} %get-tuple-element.13), channel_id=1, source_target_pairs={{0,1},{1,2},{2,3},{3,4},{4,5},{5,6},{6,7},{7,8},{8,9},{9,10},{10,1... | collective-permute-start | bytes 12296 | tf_op jit(solution)/shard_map/ppermute | solution.py:33
  11.0 5.2 %collective-permute-start.1 = (bf16[2,1024]{1,0:T(2,128)(2,1)S(1)}, bf16[2,1024]{1,0:T(2,128)(2,1)S(1)}, u32[]{:S(2)}, u32[]{:S(2)}) collective-permute-start(bf16[2,1024]{1,0:T(2,128)(2,1)S(1)} %get-tuple-element.14), channel_id=1, source_target_pairs={{1,0},{2,1},{3,2},{4,3},{5,4},{6,5},{7,6},{8,7},{9,8},{10,9},{11,1... | collective-permute-start | bytes 12296 | tf_op jit(solution)/shard_map/ppermute | solution.py:34
  16.5 9.0 %collective-permute-start.2 = (bf16[16,4096]{1,0:T(8,128)(2,1)S(1)}, bf16[16,4096]{1,0:T(8,128)(2,1)S(1)}, u32[]{:S(2)}, u32[]{:S(2)}) collective-permute-start(bf16[16,4096]{1,0:T(8,128)(2,1)S(1)} %reshape.38), channel_id=1, source_target_pairs={{0,2},{2,4},{4,6},{6,8},{8,10},{10,12},{12,14},{14,0},{1,3},{3,5},... | collective-permute-start | bytes 393224 | tf_op jit(solution)/shard_map/ppermute | solution.py:19
  25.4 8.8 %collective-permute-start.3 = (bf16[16,4096]{1,0:T(8,128)(2,1)S(1)}, bf16[16,4096]{1,0:T(8,128)(2,1)S(1)}, u32[]{:S(2)}, u32[]{:S(2)}) collective-permute-start(bf16[16,4096]{1,0:T(8,128)(2,1)S(1)} %collective-permute-done.2), channel_id=1, source_target_pairs={{0,2},{2,4},{4,6},{6,8},{8,10},{10,12},{12,14},{14,0},{1,3},{3,5},... | collective-permute-start | bytes 393224 | tf_op jit(solution)/shard_map/ppermute | solution.py:19
  25.4 9.1 %collective-permute-start.6 = (bf16[16,4096]{1,0:T(8,128)(2,1)S(1)}, bf16[16,4096]{1,0:T(8,128)(2,1)S(1)}, u32[]{:S(2)}, u32[]{:S(2)}) collective-permute-start(bf16[16,4096]{1,0:T(8,128)(2,1)S(1)} %reshape.38), channel_id=1, source_target_pairs={{0,14},{2,0},{4,2},{6,4},{8,6},{10,8},{12,10},{14,12},{1,15},{3,1}... | collective-permute-start | bytes 393224 | tf_op jit(solution)/shard_map/ppermute | solution.py:21
  34.2 7.9 %collective-permute-start.4 = (bf16[16,4096]{1,0:T(8,128)(2,1)S(1)}, bf16[16,4096]{1,0:T(8,128)(2,1)S(1)}, u32[]{:S(2)}, u32[]{:S(2)}) collective-permute-start(bf16[16,4096]{1,0:T(8,128)(2,1)S(1)} %collective-permute-done.3), channel_id=1, source_target_pairs={{0,2},{2,4},{4,6},{6,8},{8,10},{10,12},{12,14},{14,0},{1,3},{3,5},... | collective-permute-start | bytes 393224 | tf_op jit(solution)/shard_map/ppermute | solution.py:19
  34.5 8.2 %collective-permute-start.7 = (bf16[16,4096]{1,0:T(8,128)(2,1)S(1)}, bf16[16,4096]{1,0:T(8,128)(2,1)S(1)}, u32[]{:S(2)}, u32[]{:S(2)}) collective-permute-start(bf16[16,4096]{1,0:T(8,128)(2,1)S(1)} %collective-permute-done.6), channel_id=1, source_target_pairs={{0,14},{2,0},{4,2},{6,4},{8,6},{10,8},{12,10},{14,12},{1,15},{3,1}... | collective-permute-start | bytes 393224 | tf_op jit(solution)/shard_map/ppermute | solution.py:21
  42.1 7.8 %collective-permute-start.5 = (bf16[16,4096]{1,0:T(8,128)(2,1)S(1)}, bf16[16,4096]{1,0:T(8,128)(2,1)S(1)}, u32[]{:S(2)}, u32[]{:S(2)}) collective-permute-start(bf16[16,4096]{1,0:T(8,128)(2,1)S(1)} %collective-permute-done.4), channel_id=1, source_target_pairs={{0,2},{2,4},{4,6},{6,8},{8,10},{10,12},{12,14},{14,0},{1,3},{3,5},... | collective-permute-start | bytes 393224 | tf_op jit(solution)/shard_map/ppermute | solution.py:19
  42.7 7.6 %collective-permute-start.8 = (bf16[16,4096]{1,0:T(8,128)(2,1)S(1)}, bf16[16,4096]{1,0:T(8,128)(2,1)S(1)}, u32[]{:S(2)}, u32[]{:S(2)}) collective-permute-start(bf16[16,4096]{1,0:T(8,128)(2,1)S(1)} %collective-permute-done.7), channel_id=1, source_target_pairs={{0,14},{2,0},{4,2},{6,4},{8,6},{10,8},{12,10},{14,12},{1,15},{3,1}... | collective-permute-start | bytes 393224 | tf_op jit(solution)/shard_map/ppermute | solution.py:21
  50.5 45.8 %copy-start.3 = (f32[4096]{0:T(1024)S(1)}, f32[4096]{0:T(1024)}, u32[]{:S(2)}) copy-start(f32[4096]{0:T(1024)} %param.12) | copy-start | bytes 49156
  54.2 120.9 %reduce-scatter.3.cloned.1.call-start = ((), (), s32[]{:S(2)}) async-start(), calls=%async_computation.3 | async-start | bytes 1179648 | tf_op jit(solution)/shard_map/reduce_scatter | solution.py:107
  96.3 3.4 %copy-start.2 = (bf16[128,4096]{1,0:T(8,128)(2,1)S(1)}, bf16[128,4096]{1,0:T(8,128)(2,1)}, u32[]{:S(2)}) copy-start(bf16[128,4096]{1,0:T(8,128)(2,1)} %all-gather.2.cloned.1.call-done) | copy-start | bytes 3145732
  99.7 6.7 %collective-permute-start.10 = (bf16[128,512]{1,0:T(8,128)(2,1)S(1)}, bf16[128,512]{1,0:T(8,128)(2,1)S(1)}, u32[]{:S(2)}, u32[]{:S(2)}) collective-permute-start(bf16[128,512]{1,0:T(8,128)(2,1)S(1)} %fusion.21), channel_id=1, source_target_pairs={{0,1},{1,0},{2,3},{3,2},{4,5},{5,4},{6,7},{7,6},{8,9},{9,8},{10,11... | collective-permute-start | bytes 393224 | tf_op jit(solution)/shard_map/ppermute | solution.py:42
  102.7 3.5 %collective-permute-start.9 = (bf16[128,512]{1,0:T(8,128)(2,1)S(1)}, bf16[128,512]{1,0:T(8,128)(2,1)S(1)}, u32[]{:S(2)}, u32[]{:S(2)}) collective-permute-start(bf16[128,512]{1,0:T(8,128)(2,1)S(1)} %fusion.15), channel_id=1, source_target_pairs={{0,1},{1,0},{2,3},{3,2},{4,5},{5,4},{6,7},{7,6},{8,9},{9,8},{10,11... | collective-permute-start | bytes 393224 | tf_op jit(solution)/shard_map/ppermute | solution.py:42
  108.1 67.0 %copy-start = (bf16[128,512]{1,0:T(8,128)(2,1)S(1)}, bf16[128,512]{1,0:T(8,128)(2,1)}, u32[]{:S(2)}) copy-start(bf16[128,512]{1,0:T(8,128)(2,1)} %convolution_convert_fusion.2) | copy-start | bytes 393220
  112.1 134.3 %reduce-scatter.5.cloned.1.call-start = ((), (), s32[]{:S(2)}) async-start(), calls=%async_computation.4 | async-start | bytes 2359296 | tf_op jit(solution)/shard_map/reduce_scatter | solution.py:111
  179.4 68.0 %copy-start.1 = (bf16[64,1024]{1,0:T(8,128)(2,1)S(1)}, bf16[64,1024]{1,0:T(8,128)(2,1)}, u32[]{:S(2)}) copy-start(bf16[64,1024]{1,0:T(8,128)(2,1)} %param.8) | copy-start | bytes 393220
Sparse Core Ops, SparseCore 0:
  54.3 40.4 all-gather.1
  112.2 62.8 reduce-scatter.2
  179.6 66.7 reduce-scatter.4
